TPU v7x, 32 devices: a whole 2x2x4 slice. The times are simulated.
32 devices in a mesh: pencil: 8 (over z, y), angle: 4 (over x, core).
Axes of the slice: x: 2, y: 2, z: 4, core: 2. Of those that a mesh axis runs over, the one named last changes fastest.
Arguments:
- tomo_real: bfloat16 [512, 512, 128], P(None, 'pencil'), may hold values from -6 to 6
- tomo_imag: bfloat16 [512, 512, 128], P(None, 'pencil'), may hold values from -6 to 6
- template_real: bfloat16 [8, 512, 512, 128], P('angle', None, 'pencil'), may hold values from -6 to 6
- template_imag: bfloat16 [8, 512, 512, 128], P('angle', None, 'pencil'), may hold values from -6 to 6
- wedge_flags: int32 [512, 512, 128], P(None, 'pencil'), may hold values 0 or 1
- local_sigma: float32 [512, 512, 128], P('pencil'), may hold values from 0.5 to 2
Outputs:
- best_score: float32 [512, 512, 128], P('pencil', 'angle')
- runner_up: float32 [512, 512, 128], P('pencil', 'angle')
All inputs are finite; a program needn't handle non-finite values. No bound on the sum of `wedge_flags` on one device may be relied on, other than what follows from the above.
Results may differ from a plain program's by a relative error of at most 0.0064.
Values may be sent and summed in bfloat16 or wider, within the bound.
A program may use at most 256 MiB of HBM per device.

v0:
```python
import math

import jax
import jax.numpy as jnp
from jax import lax
from jax.sharding import PartitionSpec as P


def make_tables(length):
    positions = jnp.arange(length, dtype=jnp.int32)
    products = positions[:, None] * positions[None, :] % length
    phases = products.astype(jnp.float32) * (2.0 * math.pi / length)
    return (jnp.cos(phases).astype(jnp.bfloat16), jnp.sin(phases).astype(jnp.bfloat16))


def combine_top(first, later):
    return (
        jnp.maximum(first[0], later[0]),
        jnp.maximum(jnp.minimum(first[0], later[0]), jnp.maximum(first[1], later[1])),
    )


def on_device(tomo_real, tomo_imag, template_real, template_imag, wedge_flags, local_sigma):
    size_x, rows_y, size_z = tomo_real.shape
    angle_count = template_real.shape[0]
    size_y = local_sigma.shape[1]
    cos_z, sin_z = make_tables(size_z)
    cos_x, sin_x = make_tables(size_x)
    cos_y, sin_y = make_tables(size_y)
    flags = wedge_flags.astype(jnp.float32)
    spec_real = tomo_real.astype(jnp.float32)
    spec_imag = tomo_imag.astype(jnp.float32)
    norm_scale = 1.0 / math.sqrt(size_x * size_y * size_z)
    best_score = jnp.full(local_sigma.shape, -1e30, dtype=jnp.float32)
    runner_up = best_score
    for angle_slot in range(angle_count):
        temp_real = template_real[angle_slot].astype(jnp.float32)
        temp_imag = template_imag[angle_slot].astype(jnp.float32)
        prod_real = (
            (flags * (spec_real * temp_real + spec_imag * temp_imag))
            .astype(jnp.bfloat16)
            .reshape(size_x * rows_y, size_z)
        )
        prod_imag = (
            (flags * (spec_imag * temp_real - spec_real * temp_imag))
            .astype(jnp.bfloat16)
            .reshape(size_x * rows_y, size_z)
        )
        first_real = (
            (
                jnp.dot(prod_real, cos_z, preferred_element_type=jnp.float32)
                - jnp.dot(prod_imag, sin_z, preferred_element_type=jnp.float32)
            )
            .astype(jnp.bfloat16)
            .reshape(size_x, rows_y * size_z)
        )
        first_imag = (
            (
                jnp.dot(prod_real, sin_z, preferred_element_type=jnp.float32)
                + jnp.dot(prod_imag, cos_z, preferred_element_type=jnp.float32)
            )
            .astype(jnp.bfloat16)
            .reshape(size_x, rows_y * size_z)
        )
        second_real = (
            jnp.dot(cos_x, first_real, preferred_element_type=jnp.float32)
            - jnp.dot(sin_x, first_imag, preferred_element_type=jnp.float32)
        ).astype(jnp.bfloat16)
        second_imag = (
            jnp.dot(sin_x, first_real, preferred_element_type=jnp.float32)
            + jnp.dot(cos_x, first_imag, preferred_element_type=jnp.float32)
        ).astype(jnp.bfloat16)
        moved_real = second_real.reshape(size_x, rows_y, size_z)
        moved_imag = second_imag.reshape(size_x, rows_y, size_z)
        part_real = jnp.einsum(
            "ky,xkz->xyz",
            cos_y,
            lax.all_to_all(moved_real, "pencil", split_axis=0, concat_axis=1, tiled=True),
            preferred_element_type=jnp.float32,
        )
        part_imag = jnp.einsum(
            "ky,xkz->xyz",
            sin_y,
            lax.all_to_all(moved_imag, "pencil", split_axis=0, concat_axis=1, tiled=True),
            preferred_element_type=jnp.float32,
        )
        correlation = (part_real - part_imag) * norm_scale
        scores = correlation / local_sigma
        best_score, runner_up = combine_top(
            (best_score, runner_up), (scores, jnp.full_like(scores, -1e30))
        )
    got_best, got_runner = (
        lax.all_to_all(
            best_score[None].astype(jnp.bfloat16), "angle", split_axis=2, concat_axis=0, tiled=True
        ).astype(jnp.float32),
        lax.all_to_all(
            runner_up[None].astype(jnp.bfloat16), "angle", split_axis=2, concat_axis=0, tiled=True
        ).astype(jnp.float32),
    )
    best_out, runner_out = (got_best[0], got_runner[0])
    for group_slot in range(1, lax.axis_size("angle")):
        best_out, runner_out = combine_top(
            (best_out, runner_out), (got_best[group_slot], got_runner[group_slot])
        )
    return (best_out, runner_out)


def solution(mesh):
    in_specs = (
        P(None, "pencil", None),
        P(None, "pencil", None),
        P("angle", None, "pencil", None),
        P("angle", None, "pencil", None),
        P(None, "pencil", None),
        P("pencil", None, None),
    )
    out_specs = (P("pencil", "angle", None), P("pencil", "angle", None))
    return jax.shard_map(
        on_device, mesh=mesh, in_specs=in_specs, out_specs=out_specs, check_vma=False
    )
```

profile of v0, /device:TPU:9, one launch (start us, length us, event | category | flops | bytes accessed | tf_op | source)
XLA Modules:
  0.0 1242.8 jit_solution(5413188484026074353)
XLA Ops:
  0.6 36.3 %fusion.9 = (bf16[512,64,128]{2,1,0:T(8,128)(2,1)}, bf16[512,64,128]{2,1,0:T(8,128)(2,1)}, bf16[512,64,128]{2,1,0:T(8,128)(2,1)}, bf16[512,64,128]{2,1,0:T(8,128)(2,1)}) fusion(bf16[512,64,128]{2,1,0:T(8,128)(2,1)} %param.6, bf16[512,64,128]{2,1,0:T(8,128)(2,1)} %param.7, s32[512,64,128]{2,1,0:T(8,128)} %param.10, bf16[2,512,64,128]{3,2,1,0:T(8,128)(2,1)} %param.9, ...), kind=kLoop, calls=%fused_computation.21 | loop fusion | flops 113246208 | bytes 100663296 | tf_op jit(solution)/shard_map/convert_element_type | solution.py:46
  83.8 14.0 %fusion.1 = bf16[32768,128]{1,0:T(8,128)(2,1)} fusion(f32[32768,128]{1,0:T(8,128)} %fusion.48, bf16[32768,128]{1,0:T(8,128)(2,1)} %bitcast.105), kind=kOutput, calls=%fused_computation.3 | convolution fusion | flops 1082376192 | bytes 33554432 | tf_op jit(solution)/shard_map/dot_general | solution.py:52
  111.1 15.0 %fusion.40 = f32[512,8192]{1,0:T(8,128)} fusion(bf16[512,8192]{1,0:T(8,128)(2,1)} %reshape.91), kind=kOutput, calls=%fused_computation.73 | convolution fusion | flops 4298899456 | bytes 25165824 | tf_op jit(solution)/shard_map/dot_general | solution.py:70
  126.1 16.4 %fusion.21 = bf16[64,8,64,128]{3,1,2,0:T(8,128)(2,1)} fusion(f32[512,8192]{1,0:T(8,128)} %fusion.40, bf16[512,8192]{1,0:T(8,128)(2,1)} %reshape.92), kind=kOutput, calls=%fused_computation.43 | convolution fusion | flops 4307288064 | bytes 33554432 | tf_op jit(solution)/shard_map/dot_general | solution.py:71
  157.5 15.0 %fusion.38 = f32[512,8192]{1,0:T(8,128)} fusion(bf16[512,8192]{1,0:T(8,128)(2,1)} %reshape.91), kind=kOutput, calls=%fused_computation.71 | convolution fusion | flops 4298899456 | bytes 25165824 | tf_op jit(solution)/shard_map/dot_general | solution.py:66
  172.5 16.3 %fusion.20 = bf16[64,8,64,128]{3,1,2,0:T(8,128)(2,1)} fusion(f32[512,8192]{1,0:T(8,128)} %fusion.38, bf16[512,8192]{1,0:T(8,128)(2,1)} %reshape.92), kind=kOutput, calls=%fused_computation.42 | convolution fusion | flops 4307288064 | bytes 33554432 | tf_op jit(solution)/shard_map/dot_general | solution.py:67
  198.1 140.8 %all-to-all-done.3 = bf16[512,64,128]{2,1,0:T(8,128)(2,1)} async-done(((bf16[512,64,128]{2,1,0:T(8,128)(2,1)}), bf16[512,64,128]{2,1,0:T(8,128)(2,1)}, u32[]{:S(2)}, u32[]{:S(2)}) %all-to-all-start.3) | async-done | bytes 8388640 | tf_op jit(solution)/shard_map/all_to_all | solution.py:84
  356.8 14.0 %fusion.2 = bf16[32768,128]{1,0:T(8,128)(2,1)} fusion(f32[32768,128]{1,0:T(8,128)} %fusion.51, bf16[32768,128]{1,0:T(8,128)(2,1)} %bitcast.102), kind=kOutput, calls=%fused_computation.5 | convolution fusion | flops 1082376192 | bytes 33554432 | tf_op jit(solution)/shard_map/dot_general | solution.py:60
  423.1 15.4 %fusion.41 = f32[512,8192]{1,0:T(8,128)} fusion(bf16[512,8192]{1,0:T(8,128)(2,1)} %reshape.85), kind=kOutput, calls=%fused_computation.74 | convolution fusion | flops 4298899456 | bytes 25165824 | tf_op jit(solution)/shard_map/dot_general | solution.py:70
  438.4 16.3 %fusion.19 = bf16[64,8,64,128]{3,1,2,0:T(8,128)(2,1)} fusion(f32[512,8192]{1,0:T(8,128)} %fusion.41, bf16[512,8192]{1,0:T(8,128)(2,1)} %reshape.86), kind=kOutput, calls=%fused_computation.41 | convolution fusion | flops 4307288064 | bytes 33554432 | tf_op jit(solution)/shard_map/dot_general | solution.py:71
  464.0 62.4 %all-to-all-done.2 = bf16[512,64,128]{2,1,0:T(8,128)(2,1)} async-done(((bf16[512,64,128]{2,1,0:T(8,128)(2,1)}), bf16[512,64,128]{2,1,0:T(8,128)(2,1)}, u32[]{:S(2)}, u32[]{:S(2)}) %all-to-all-start.2) | async-done | bytes 8388640 | tf_op jit(solution)/shard_map/all_to_all | solution.py:78
  532.2 15.0 %fusion.39 = f32[512,8192]{1,0:T(8,128)} fusion(bf16[512,8192]{1,0:T(8,128)(2,1)} %reshape.85), kind=kOutput, calls=%fused_computation.72 | convolution fusion | flops 4298899456 | bytes 25165824 | tf_op jit(solution)/shard_map/dot_general | solution.py:66
  547.2 16.3 %fusion.18 = bf16[64,8,64,128]{3,1,2,0:T(8,128)(2,1)} fusion(f32[512,8192]{1,0:T(8,128)} %fusion.39, bf16[512,8192]{1,0:T(8,128)(2,1)} %reshape.86), kind=kOutput, calls=%fused_computation.40 | convolution fusion | flops 4307288064 | bytes 33554432 | tf_op jit(solution)/shard_map/dot_general | solution.py:67
  572.8 140.9 %all-to-all-done.1 = bf16[512,64,128]{2,1,0:T(8,128)(2,1)} async-done(((bf16[512,64,128]{2,1,0:T(8,128)(2,1)}), bf16[512,64,128]{2,1,0:T(8,128)(2,1)}, u32[]{:S(2)}, u32[]{:S(2)}) %all-to-all-start.1) | async-done | bytes 8388640 | tf_op jit(solution)/shard_map/all_to_all | solution.py:84
  719.6 17.5 %copy.40 = f32[64,512,128]{1,2,0:T(8,128)} copy(f32[64,512,128]{2,1,0:T(8,128)} %param.11) | data formatting | bytes 33554432 | tf_op args[5]
  765.9 15.6 %fusion.34 = f32[64,128,512]{2,1,0:T(8,128)} fusion(bf16[64,512,128]{2,1,0:T(8,128)(2,1)} %bitcast.110), kind=kOutput, calls=%fused_computation.67 | convolution fusion | flops 4298899456 | bytes 25165824 | tf_op jit(solution)/shard_map/ky,xkz->xyz/dot_general | solution.py:75
  781.5 119.6 %all-to-all-done = bf16[512,64,128]{2,1,0:T(8,128)(2,1)} async-done(((bf16[512,64,128]{2,1,0:T(8,128)(2,1)}), bf16[512,64,128]{2,1,0:T(8,128)(2,1)}, u32[]{:S(2)}, u32[]{:S(2)}) %all-to-all-start) | async-done | bytes 8388640 | tf_op jit(solution)/shard_map/all_to_all | solution.py:78
  910.8 15.4 %fusion.36 = f32[64,128,512]{2,1,0:T(8,128)} fusion(bf16[64,512,128]{2,1,0:T(8,128)(2,1)} %bitcast.111), kind=kOutput, calls=%fused_computation.69 | convolution fusion | flops 4298899456 | bytes 25165824 | tf_op jit(solution)/shard_map/ky,xkz->xyz/dot_general | solution.py:75
  926.2 19.6 %bitcast_divide_fusion = bf16[64,512,128]{1,2,0:T(8,128)(2,1)} fusion(f32[64,512,128]{1,2,0:T(8,128)} %copy.40, f32[64,128,512]{2,1,0:T(8,128)S(1)} %copy-done.1, bf16[64,512,128]{2,1,0:T(8,128)(2,1)} %bitcast.117), kind=kOutput, calls=%fused_computation.28 | convolution fusion | flops 4315676672 | bytes 50331648 | tf_op jit(solution)/shard_map/ky,xkz->xyz/dot_general | solution.py:81
  945.7 27.1 %fusion.17 = (bf16[1,64,512,128]{2,3,1,0:T(8,128)(2,1)}, bf16[1,64,512,128]{2,3,1,0:T(8,128)(2,1)}) fusion(bf16[64,512,128]{1,2,0:T(8,128)(2,1)} %bitcast_divide_fusion, f32[64,512,128]{1,2,0:T(8,128)} %copy.40, f32[64,128,512]{2,1,0:T(8,128)} %fusion.36, bf16[64,512,128]{2,1,0:T(8,128)(2,1)} %bitcast.116), kind=kOutput, calls=%fused_computation.39 | convolution fusion | flops 4349231104 | bytes 67108864 | tf_op jit(solution)/shard_map/ky,xkz->xyz/dot_general | solution.py:81
  1003.0 80.2 %all-to-all-done.5 = bf16[1,64,512,128]{3,1,0,2:T(8,128)(2,1)} async-done(((bf16[1,64,512,128]{3,1,0,2:T(8,128)(2,1)}), bf16[1,64,512,128]{3,1,0,2:T(8,128)(2,1)}, u32[]{:S(2)}, u32[]{:S(2)}) %all-to-all-start.5) | async-done | bytes 8388640 | tf_op jit(solution)/shard_map/all_to_all | solution.py:96
  1101.3 80.9 %all-to-all-done.4 = bf16[1,64,512,128]{3,1,0,2:T(8,128)(2,1)} async-done(((bf16[1,64,512,128]{3,1,0,2:T(8,128)(2,1)}), bf16[1,64,512,128]{3,1,0,2:T(8,128)(2,1)}, u32[]{:S(2)}, u32[]{:S(2)}) %all-to-all-start.4) | async-done | bytes 8388640 | tf_op jit(solution)/shard_map/all_to_all | solution.py:93
  1193.5 32.6 %copy_bitcast_fusion = (f32[4,1,64,128,128]{4,3,2,1,0:T(8,128)}, f32[4,1,64,128,128]{4,3,2,1,0:T(8,128)}) fusion(f32[1,64,4,128,128]{4,1,3,2,0:T(8,128)} %convert.13, f32[1,64,4,128,128]{4,1,3,2,0:T(8,128)} %convert.12), kind=kLoop, calls=%fused_computation.30 | loop fusion | bytes 67108864 | tf_op jit(solution)/shard_map/convert_element_type | solution.py:98
  1226.1 16.5 %fusion.23 = (f32[64,128,128]{2,1,0:T(8,128)}, f32[64,128,128]{2,1,0:T(8,128)}) fusion(f32[4,1,64,128,128]{4,3,2,1,0:T(8,128)} %get-tuple-element.10, f32[4,1,64,128,128]{4,3,2,1,0:T(8,128)} %get-tuple-element.11), kind=kLoop, calls=%fused_computation.46 | loop fusion | flops 12582912 | bytes 41943040 | tf_op jit(solution)/shard_map/max | solution.py:19
  (32 shorter events, 282.9 us)
Async XLA Ops:
  37.0 11.8 copy-start
  151.8 187.1 %all-to-all-start.3 = ((bf16[512,64,128]{2,1,0:T(8,128)(2,1)}), bf16[512,64,128]{2,1,0:T(8,128)(2,1)}, u32[]{:S(2)}, u32[]{:S(2)}) async-start(bf16[512,64,128]{2,1,0:T(8,128)(2,1)} %bitcast.115), calls=%async_computation.3 | async-start | bytes 16777216 | tf_op jit(solution)/shard_map/all_to_all | solution.py:84
  338.9 187.5 %all-to-all-start.2 = ((bf16[512,64,128]{2,1,0:T(8,128)(2,1)}), bf16[512,64,128]{2,1,0:T(8,128)(2,1)}, u32[]{:S(2)}, u32[]{:S(2)}) async-start(bf16[512,64,128]{2,1,0:T(8,128)(2,1)} %bitcast.112), calls=%async_computation.2 | async-start | bytes 16777216 | tf_op jit(solution)/shard_map/all_to_all | solution.py:78
  526.4 187.4 %all-to-all-start.1 = ((bf16[512,64,128]{2,1,0:T(8,128)(2,1)}), bf16[512,64,128]{2,1,0:T(8,128)(2,1)}, u32[]{:S(2)}, u32[]{:S(2)}) async-start(bf16[512,64,128]{2,1,0:T(8,128)(2,1)} %bitcast.114), calls=%async_computation.1 | async-start | bytes 16777216 | tf_op jit(solution)/shard_map/all_to_all | solution.py:84
  713.7 187.4 %all-to-all-start = ((bf16[512,64,128]{2,1,0:T(8,128)(2,1)}), bf16[512,64,128]{2,1,0:T(8,128)(2,1)}, u32[]{:S(2)}, u32[]{:S(2)}) async-start(bf16[512,64,128]{2,1,0:T(8,128)(2,1)} %bitcast.113), calls=%async_computation | async-start | bytes 16777216 | tf_op jit(solution)/shard_map/all_to_all | solution.py:78
  910.8 15.4 %copy-start.1 = (f32[64,128,512]{2,1,0:T(8,128)S(1)}, f32[64,128,512]{2,1,0:T(8,128)}, u32[]{:S(2)}) copy-start(f32[64,128,512]{2,1,0:T(8,128)} %fusion.34) | copy-start | bytes 50331652
  985.0 98.3 %all-to-all-start.5 = ((bf16[1,64,512,128]{3,1,0,2:T(8,128)(2,1)}), bf16[1,64,512,128]{3,1,0,2:T(8,128)(2,1)}, u32[]{:S(2)}, u32[]{:S(2)}) async-start(bf16[1,64,512,128]{3,1,0,2:T(8,128)(2,1)} %copy.48), calls=%async_computation.5 | async-start | bytes 16777216 | tf_op jit(solution)/shard_map/all_to_all | solution.py:96
  1083.3 98.9 %all-to-all-start.4 = ((bf16[1,64,512,128]{3,1,0,2:T(8,128)(2,1)}), bf16[1,64,512,128]{3,1,0,2:T(8,128)(2,1)}, u32[]{:S(2)}, u32[]{:S(2)}) async-start(bf16[1,64,512,128]{3,1,0,2:T(8,128)(2,1)} %copy.46), calls=%async_computation.4 | async-start | bytes 16777216 | tf_op jit(solution)/shard_map/all_to_all | solution.py:93
where the time goes:
time: 1260 us; the launch traced here: 1240 us
  waiting for transfers between devices  625 us (50%)
  matrix products  302 us (24%)
  local copies, waits for them, and re-layouts  204 us (16%)
  other arithmetic  75.4 us (6%)
  starting transfers between devices  36.4 us (3%)
    all_to_all x2, waiting for transfers between devices, on_device(): lax.all_to_all(moved_imag, 'pencil', split_axis=0, concat_axis=1, tiled=T...  282 us
    all_to_all x2, waiting for transfers between devices, on_device(): lax.all_to_all(moved_real, 'pencil', split_axis=0, concat_axis=1, tiled=T...  182 us
    all_to_all x1, waiting for transfers between devices, on_device(): lax.all_to_all(best_score[None].astype(jnp.bfloat16), 'angle', split_axis...  80.9 us
    all_to_all x1, waiting for transfers between devices, on_device(): lax.all_to_all(runner_up[None].astype(jnp.bfloat16), 'angle', split_axis=...  80.2 us
    unnamed x9, local copies, waits for them, and re-layouts  54.7 us
    dot_general x2, matrix products, on_device(): jnp.einsum('ky,xkz->xyz', sin_y, lax.all_to_all(moved_imag, 'pencil', spl...  46.7 us
    convert_element_type x1, other arithmetic, on_device(): prod_imag = (flags * (spec_imag * temp_real - spec_real * temp_imag)).ast...  36.3 us
    dot_general x2, matrix products, on_device(): jnp.dot(cos_x, first_imag, preferred_element_type=jnp.float32)  32.7 us
  transfers between devices with their start and end apart: 6, of which 6 were waited for; matrix products, arithmetic and copies ran while one was open for 23% of the time, Pallas kernels for 0%

commit v1 on v0

v1 whole, which is shorter than its diff:
```python
import functools
import math

import jax
import jax.numpy as jnp
import numpy as np
from jax import lax
from jax.experimental import pallas as pl
from jax.experimental.pallas import tpu as pltpu
from jax.sharding import PartitionSpec as P

MESH = pl.DeviceIdType.MESH
KY_ROWS = 8
X_ROWS = 4
SLOTS = 8
AHEAD = 3


def make_tables(length):
    positions = np.arange(length, dtype=np.int64)
    products = positions[:, None] * positions[None, :] % length
    phases = products.astype(np.float32) * np.float32(2.0 * math.pi / length)
    return np.cos(phases), np.sin(phases)


def combine_top(first, later):
    return (
        jnp.maximum(first[0], later[0]),
        jnp.maximum(jnp.minimum(first[0], later[0]), jnp.maximum(first[1], later[1])),
    )


def kernel(
    dims,
    tomo_r, tomo_i, temp_r, temp_i, flags, sigma, table_z, table_x, table_y,
    spec_out, recv, tops,
    tr_buf, ti_buf, fl_buf, pr_buf, pi_buf, q_buf, r_buf, out_buf,
    tz, wx, wy, in_buf, sig_buf, top_buf,
    tab_sem, tomo_sem, temp_sem, back_sem, send_sem, early_sem, recv_sem,
    load_sem, top_sem, tops_sem,
):
    angles, size_x, rows, size_z, peers, planes, size_y, groups = dims
    me = lax.axis_index("pencil")
    my_group = lax.axis_index("angle")
    kyb = min(KY_ROWS, rows)
    n_kb = rows // kyb
    xc = min(X_ROWS, planes)
    n_chunks = planes // xc
    early = max(1, n_chunks // 4)
    y_block = size_y // groups
    slots = top_buf.shape[0]
    norm = 1.0 / math.sqrt(size_x * size_y * size_z)

    barrier = pltpu.get_barrier_semaphore()

    def greet_pencil(d, carry):
        pl.semaphore_signal(
            barrier, inc=1, device_id={"pencil": lax.rem(me + d, peers)}, device_id_type=MESH
        )
        return carry

    def greet_group(d, carry):
        pl.semaphore_signal(
            barrier, inc=1, device_id={"angle": lax.rem(my_group + d, groups)}, device_id_type=MESH
        )
        return carry

    lax.fori_loop(1, peers, greet_pencil, 0)
    lax.fori_loop(1, groups, greet_group, 0)

    tables = [
        pltpu.make_async_copy(table_z, tz, tab_sem.at[0]),
        pltpu.make_async_copy(table_x, wx, tab_sem.at[1]),
        pltpu.make_async_copy(table_y, wy, tab_sem.at[2]),
    ]

    def tomo_copies(kb, slot):
        at = (slice(None), pl.ds(pl.multiple_of(kb * kyb, kyb), kyb), slice(None))
        return [
            pltpu.make_async_copy(tomo_r.at[at], tr_buf.at[slot], tomo_sem.at[slot, 0]),
            pltpu.make_async_copy(tomo_i.at[at], ti_buf.at[slot], tomo_sem.at[slot, 1]),
            pltpu.make_async_copy(flags.at[at], fl_buf.at[slot], tomo_sem.at[slot, 2]),
        ]

    def temp_copies(kb, a, slot):
        at = (a, slice(None), pl.ds(pl.multiple_of(kb * kyb, kyb), kyb), slice(None))
        return [
            pltpu.make_async_copy(temp_r.at[at], pr_buf.at[slot], temp_sem.at[slot, 0]),
            pltpu.make_async_copy(temp_i.at[at], pi_buf.at[slot], temp_sem.at[slot, 1]),
        ]

    for copy in tomo_copies(0, 0) + temp_copies(0, 0, 0) + tables:
        copy.start()
    pl.semaphore_wait(barrier, peers - 1 + groups - 1)
    for copy in tables:
        copy.wait()

    kxc = min(64, size_x)
    xt = min(128, size_x)
    width = planes * early // n_chunks

    def transform(kb, a, tomo_slot, temp_slot):
        def product(j, carry):
            at = pl.ds(pl.multiple_of(j * kxc, kxc), kxc)
            flag = fl_buf[tomo_slot, at].astype(jnp.float32)
            sr = tr_buf[tomo_slot, at].astype(jnp.float32)
            si = ti_buf[tomo_slot, at].astype(jnp.float32)
            pr = pr_buf[temp_slot, at].astype(jnp.float32)
            pi = pi_buf[temp_slot, at].astype(jnp.float32)
            prod_r = (flag * (sr * pr + si * pi)).reshape(kxc * kyb, size_z).astype(jnp.bfloat16)
            prod_i = (flag * (si * pr - sr * pi)).reshape(kxc * kyb, size_z).astype(jnp.bfloat16)
            both = jnp.concatenate([prod_r, prod_i], axis=1)
            to = pl.ds(pl.multiple_of(j * kxc * kyb, kxc * kyb), kxc * kyb)
            first = jnp.dot(both, tz[...], preferred_element_type=jnp.float32)
            q_buf[0, to, :] = first[:, :size_z]
            q_buf[1, to, :] = first[:, size_z:]
            return carry

        lax.fori_loop(0, size_x // kxc, product, 0)

        def along_x(ky, carry):
            at = pl.ds(ky, size_x, stride=kyb)
            q = jnp.concatenate(
                [q_buf.at[0][at, :].astype(jnp.bfloat16), q_buf.at[1][at, :].astype(jnp.bfloat16)],
                axis=1,
            )
            for t in range(size_x // xt):
                c = jnp.dot(wx[t * xt:(t + 1) * xt, :], q, preferred_element_type=jnp.float32)
                s = jnp.dot(
                    wx[size_x + t * xt:size_x + (t + 1) * xt, :], q,
                    preferred_element_type=jnp.float32,
                )
                to = pl.ds(t * xt * kyb + ky, xt, stride=kyb)
                r_buf.at[0][to, :] = c[:, :size_z] - s[:, size_z:]
                r_buf.at[1][to, :] = s[:, :size_z] + c[:, size_z:]
            return carry

        lax.fori_loop(0, kyb, along_x, 0)

        def settle(j, carry):
            at = pl.ds(pl.multiple_of(j * kxc * kyb, kxc * kyb), kxc * kyb)
            to = pl.ds(pl.multiple_of(j * kxc, kxc), kxc)
            for part in range(2):
                out_buf[part, to] = (
                    r_buf[part, at, :].reshape(kxc, kyb, size_z).astype(jnp.bfloat16)
                )
            return carry

        lax.fori_loop(0, size_x // kxc, settle, 0)

    def send_early(kb, a):
        here = pl.ds(pl.multiple_of(kb * kyb, kyb), kyb)
        there = pl.ds(pl.multiple_of(me * rows + kb * kyb, kyb), kyb)

        def one(d, carry):
            to = lax.rem(me + d, peers)
            pltpu.make_async_remote_copy(
                src_ref=spec_out.at[a, :, pl.ds(to * planes, width), here, :],
                dst_ref=recv.at[a, :, pl.ds(0, width), there, :],
                send_sem=send_sem,
                recv_sem=early_sem,
                device_id={"pencil": to},
                device_id_type=MESH,
            ).start()
            return carry

        lax.fori_loop(1, peers, one, 0)

    def step(t, carry):
        kb, a = t // angles, lax.rem(t, angles)
        tomo_slot, temp_slot = lax.rem(kb, 2), lax.rem(t, 2)

        @pl.when(a == 0)
        def _():
            for copy in tomo_copies(kb, tomo_slot):
                copy.wait()

            @pl.when(kb + 1 < n_kb)
            def _():
                for copy in tomo_copies(kb + 1, 1 - tomo_slot):
                    copy.start()

        for copy in temp_copies(kb, a, temp_slot):
            copy.wait()

        @pl.when(t + 1 < n_kb * angles)
        def _():
            for copy in temp_copies((t + 1) // angles, lax.rem(t + 1, angles), 1 - temp_slot):
                copy.start()

        transform(kb, a, tomo_slot, temp_slot)
        here = pl.ds(pl.multiple_of(kb * kyb, kyb), kyb)
        own = pl.ds(pl.multiple_of(me * rows + kb * kyb, kyb), kyb)
        back = [
            pltpu.make_async_copy(out_buf, spec_out.at[a, :, :, here, :], back_sem.at[0]),
            pltpu.make_async_copy(
                out_buf.at[:, pl.ds(me * planes, planes)], recv.at[a, :, :, own, :], back_sem.at[1]
            ),
        ]
        for copy in back:
            copy.start()
        for copy in back:
            copy.wait()
        send_early(kb, a)
        return carry

    lax.fori_loop(0, n_kb * angles, step, 0)

    def send_chunk(c):
        mine = pl.ds(me * rows, rows)

        def one(d, carry):
            to = lax.rem(me + d, peers)
            pltpu.make_async_remote_copy(
                src_ref=spec_out.at[:, :, pl.ds(to * planes + c * xc, xc), :, :],
                dst_ref=recv.at[:, :, pl.ds(c * xc, xc), mine, :],
                send_sem=send_sem,
                recv_sem=recv_sem.at[c],
                device_id={"pencil": to},
                device_id_type=MESH,
            ).start()
            return carry

        lax.fori_loop(1, peers, one, 0)

    others = pl.ds(0, (peers - 1) * rows)

    def slot_copy(slot):
        return pltpu.make_async_copy(top_buf.at[slot], top_buf.at[slot], top_sem.at[slot])

    def score(c):
        load = pltpu.make_async_copy(
            recv.at[:, :, pl.ds(c * xc, xc), :, :], in_buf, load_sem.at[1]
        )
        load.start()
        load.wait()
        pltpu.make_async_copy(sigma.at[pl.ds(c * xc, xc)], sig_buf, load_sem.at[0]).wait()

        def plane(j, carry):
            x = c * xc + j
            slot = lax.rem(x, slots)

            @pl.when(x >= slots)
            def _():
                slot_copy(slot).wait()

            sides = [
                jnp.concatenate([in_buf[a, part, j] for a in range(angles)], axis=1)
                for part in range(2)
            ]
            corr = jnp.dot(wy[:, :size_y], sides[0], preferred_element_type=jnp.float32)
            corr = corr + jnp.dot(wy[:, size_y:], sides[1], preferred_element_type=jnp.float32)
            sig = sig_buf[j]
            best = corr[:, :size_z] * norm / sig
            runner = jnp.full_like(best, -1e30)
            for a in range(1, angles):
                later = corr[:, a * size_z:(a + 1) * size_z] * norm / sig
                runner = jnp.maximum(runner, jnp.minimum(best, later))
                best = jnp.maximum(best, later)
            top_buf[slot, 0] = best.astype(jnp.bfloat16)
            top_buf[slot, 1] = runner.astype(jnp.bfloat16)

            def one(d, carry):
                to = lax.rem(my_group + d, groups)
                pltpu.make_async_remote_copy(
                    src_ref=top_buf.at[slot, :, pl.ds(pl.multiple_of(to * y_block, y_block), y_block), :],
                    dst_ref=tops.at[my_group, :, x],
                    send_sem=top_sem.at[slot],
                    recv_sem=tops_sem,
                    device_id={"angle": to},
                    device_id_type=MESH,
                ).start()
                return carry

            lax.fori_loop(1, groups, one, 0)
            pltpu.make_async_copy(
                top_buf.at[slot, :, pl.ds(pl.multiple_of(my_group * y_block, y_block), y_block), :],
                tops.at[my_group, :, x],
                top_sem.at[slot],
            ).start()
            return carry

        lax.fori_loop(0, xc, plane, 0)

    def load_sigma(c):
        pltpu.make_async_copy(sigma.at[pl.ds(c * xc, xc)], sig_buf, load_sem.at[0]).start()

    def queue_first(c, carry):
        send_chunk(c)
        return carry

    lax.fori_loop(early, min(early + AHEAD, n_chunks), queue_first, 0)
    first = recv.at[:, :, pl.ds(0, width), others, :]
    pltpu.make_async_copy(first, first, early_sem).wait()

    def early_chunk(c, carry):
        load_sigma(c)
        score(c)
        return carry

    lax.fori_loop(0, early, early_chunk, 0)

    def late_chunk(c, carry):
        @pl.when(c + AHEAD < n_chunks)
        def _():
            send_chunk(c + AHEAD)

        load_sigma(c)
        part = recv.at[:, :, pl.ds(c * xc, xc), others, :]
        pltpu.make_async_copy(part, part, recv_sem.at[c]).wait()
        score(c)
        return carry

    lax.fori_loop(early, n_chunks, late_chunk, 0)

    def drain(slot, carry):
        slot_copy(slot).wait()
        return carry

    lax.fori_loop(0, slots, drain, 0)
    theirs = tops.at[pl.ds(0, groups - 1)]
    pltpu.make_async_copy(theirs, theirs, tops_sem).wait()
    sent = spec_out.at[:, :, pl.ds(0, (peers - 1) * planes), :, :]
    pltpu.make_async_copy(sent, sent, send_sem).wait()


def on_device(tomo_real, tomo_imag, template_real, template_imag, wedge_flags, local_sigma):
    size_x, rows, size_z = tomo_real.shape
    angles = template_real.shape[0]
    planes, size_y, _ = local_sigma.shape
    peers, groups = lax.axis_size("pencil"), lax.axis_size("angle")
    dims = (angles, size_x, rows, size_z, peers, planes, size_y, groups)
    cos_z, sin_z = make_tables(size_z)
    cos_x, sin_x = make_tables(size_x)
    cos_y, sin_y = make_tables(size_y)
    table_z = jnp.asarray(np.block([[cos_z, sin_z], [-sin_z, cos_z]]), jnp.bfloat16)
    table_x = jnp.asarray(np.concatenate([cos_x, sin_x], axis=0), jnp.bfloat16)
    table_y = jnp.asarray(np.concatenate([cos_y, -sin_y], axis=1), jnp.bfloat16)
    kyb = min(KY_ROWS, rows)
    xc = min(X_ROWS, planes)
    slots = min(SLOTS, planes)
    bf16, f32 = jnp.bfloat16, jnp.float32
    hbm = pl.BlockSpec(memory_space=pl.ANY)
    dma = pltpu.SemaphoreType.DMA
    _, _, tops = pl.pallas_call(
        functools.partial(kernel, dims),
        out_shape=(
            jax.ShapeDtypeStruct((angles, 2, size_x, rows, size_z), bf16),
            jax.ShapeDtypeStruct((angles, 2, planes, peers * rows, size_z), bf16),
            jax.ShapeDtypeStruct((groups, 2, planes, size_y // groups, size_z), bf16),
        ),
        in_specs=[hbm] * 9,
        out_specs=(hbm, hbm, hbm),
        scratch_shapes=[
            pltpu.VMEM((2, size_x, kyb, size_z), bf16),
            pltpu.VMEM((2, size_x, kyb, size_z), bf16),
            pltpu.VMEM((2, size_x, kyb, size_z), jnp.int32),
            pltpu.VMEM((2, size_x, kyb, size_z), bf16),
            pltpu.VMEM((2, size_x, kyb, size_z), bf16),
            pltpu.VMEM((2, size_x * kyb, size_z), f32),
            pltpu.VMEM((2, size_x * kyb, size_z), f32),
            pltpu.VMEM((2, size_x, kyb, size_z), bf16),
            pltpu.VMEM(table_z.shape, bf16),
            pltpu.VMEM(table_x.shape, bf16),
            pltpu.VMEM(table_y.shape, bf16),
            pltpu.VMEM((angles, 2, xc, peers * rows, size_z), bf16),
            pltpu.VMEM((xc, size_y, size_z), f32),
            pltpu.VMEM((slots, 2, size_y, size_z), bf16),
            dma((3,)), dma((2, 3)), dma((2, 2)), dma((2,)), dma, dma, dma((planes // xc,)),
            dma((2,)), dma((slots,)), dma,
        ],
        compiler_params=pltpu.CompilerParams(collective_id=0, has_side_effects=True),
        name="match",
    )(
        tomo_real, tomo_imag, template_real, template_imag, wedge_flags, local_sigma,
        table_z, table_x, table_y,
    )
    tops = tops.astype(f32)
    best = (tops[0, 0], tops[0, 1])
    for group in range(1, groups):
        best = combine_top(best, (tops[group, 0], tops[group, 1]))
    return best


def solution(mesh):
    in_specs = (
        P(None, "pencil", None),
        P(None, "pencil", None),
        P("angle", None, "pencil", None),
        P("angle", None, "pencil", None),
        P(None, "pencil", None),
        P("pencil", None, None),
    )
    out_specs = (P("pencil", "angle", None), P("pencil", "angle", None))
    return jax.shard_map(
        on_device, mesh=mesh, in_specs=in_specs, out_specs=out_specs, check_vma=False
    )
```

time: 1260 us -> 801 us (0.64)
  Pallas kernels: 0 us -> 757 us
  waiting for transfers between devices: 625 us -> 0 us
  matrix products: 302 us -> 0 us
  local copies, waits for them, and re-layouts: 204 us -> 0 us
  other arithmetic: 75.4 us -> 35.2 us
  starting transfers between devices: 36.4 us -> 0 us
    pallas_call x0 -> x1, Pallas kernels: none -> 757 us  [on_device(): pl.pallas_call(functools.partial(kernel, dims), out_shape=(jax.ShapeDtype...]
    all_to_all x6 -> x0, waiting for transfers between devices: 625 us -> none  [the longest x2 282 us: on_device(): lax.all_to_all(moved_imag, 'pencil', split_axis=0, concat_axis=1, tiled=T...]
    dot_general x20 -> x0, matrix products: 302 us -> none  [the longest x2 46.7 us: on_device(): jnp.einsum('ky,xkz->xyz', sin_y, lax.all_to_all(moved_imag, 'pencil', spl...]
    convert_element_type x3 -> x0, local copies, waits for them, and re-layouts: 56.7 us -> none  [the longest x1 32.6 us: on_device(): got_best, got_runner = (lax.all_to_all(best_score[None].astype(jnp.bfloat...]
    unnamed x9 -> x0, local copies, waits for them, and re-layouts: 54.7 us -> none
    reshape x4 -> x0, local copies, waits for them, and re-layouts: 53.8 us -> none  [the longest x2 27.1 us: on_device(): first_imag = (jnp.dot(prod_real, sin_z, preferred_element_type=jnp.float3...]
    convert_element_type x3 -> x1, other arithmetic: 58.9 us -> 18.7 us  [on_device(): tops = tops.astype(f32)]
    all_to_all x4 -> x0, local copies, waits for them, and re-layouts: 38.5 us -> none  [the longest x2 19.2 us: on_device(): lax.all_to_all(moved_imag, 'pencil', split_axis=0, concat_axis=1, tiled=T...]
  transfers between devices with their start and end apart: 6 -> 0, of which waited for: 6 -> 0; matrix products, arithmetic and copies ran while one was open for 23% -> 0% of each run, Pallas kernels for 0% -> 0%
where the time goes in v1:
time: 801 us; the launch traced here: 793 us
  Pallas kernels  757 us (95%)
  other arithmetic  35.2 us (4%)
    pallas_call x1, Pallas kernels, on_device(): pl.pallas_call(functools.partial(kernel, dims), out_shape=(jax.ShapeDtype...  757 us
    convert_element_type x1, other arithmetic, on_device(): tops = tops.astype(f32)  18.7 us
    max x1, other arithmetic, combine_top(): jnp.maximum(jnp.minimum(first[0], later[0]), jnp.maximum(first[1], later[...  16.5 us

profile of v1, /device:TPU:9, one launch (start us, length us, event | category | flops | bytes accessed | tf_op | source)
XLA Modules:
  0.0 793.3 jit_solution(8129108949930300469)
XLA Ops:
  0.6 757.4 %match.1 = (bf16[2,2,512,64,128]{4,3,2,1,0:T(8,128)(2,1)}, bf16[2,2,64,512,128]{4,3,2,1,0:T(8,128)(2,1)}, bf16[4,2,64,128,128]{4,3,2,1,0:T(8,128)(2,1)}) custom-call(bf16[512,64,128]{2,1,0:T(8,128)(2,1)} %tomo_r.1, bf16[512,64,128]{2,1,0:T(8,128)(2,1)} %tomo_i.1, bf16[2,512,64,128]{3,2,1,0:T(8,128)(2,1)} %temp_r.1, bf16[2,512,64,128]{3,2,1,0:T(8,128)(2,1)} %temp_i.1, ...), custom_call_target="tpu_custom_call" | custom-call | tf_op jit(solution)/shard_map/match/pallas_call | solution.py:345
  758.0 18.7 %convert_element_type.3 = f32[4,2,64,128,128]{4,3,2,1,0:T(8,128)} convert(bf16[4,2,64,128,128]{4,3,2,1,0:T(8,128)(2,1)} %get-tuple-element.3) | non-fusion elementwise | flops 8388608 | bytes 50331648 | tf_op jit(solution)/shard_map/convert_element_type | solution.py:378
  776.7 16.5 %fusion.1 = (f32[64,128,128]{2,1,0:T(8,128)}, f32[64,128,128]{2,1,0:T(8,128)}) fusion(f32[4,2,64,128,128]{4,3,2,1,0:T(8,128)} %convert_element_type.3), kind=kLoop, calls=%fused_computation.2 | loop fusion | flops 12582912 | bytes 41943040 | tf_op jit(solution)/shard_map/max | solution.py:29
